TPU v7x, 256 devices: a whole 4x4x8 slice. The times are simulated.
256 devices in a mesh: rec: 32 (over z, x), ani: 4 (over y_lo, core), chain: 2 (over y_hi).
Axes of the slice: x: 4, y: 4 (y_hi: 2, y_lo: 2; y = y_hi * 2 + y_lo), z: 8, core: 2. Of those that a mesh axis runs over, the one named last changes fastest.
Arguments:
- genotypes: bfloat16 [131072, 4096], P('ani', 'rec'), may hold values from -0.09375 to 0.09375
- effects: float32 [8192], P(('chain', 'rec')), parts along dimension 0, may hold values from -6 to 6
- gaussian_draw: float32 [8192], P(('chain', 'rec')), parts along dimension 0, may hold values from -6 to 6
- prior_prec: float32 [4096], P('rec'), may hold values from 2 to 40
- accept: int32 [64], P(('chain', 'rec')), parts along dimension 0, may hold values 0 or 1
- herd_effect: float32 [131072], P(('chain', 'rec')), parts along dimension 0, may hold values from -6 to 6
- phenotype: float32 [1048576], P(('rec', 'ani')), may hold values from -12 to 12
- record_animal: int32 [1048576], P(('rec', 'ani')), may hold values from 0 to 131071
- record_bin: int32 [1048576], P(('rec', 'ani')), may hold values from 0 to 65535, as said below
- live_records: int32 [128], P(('rec', 'ani')), may hold values from 1 to 8192, 655360 in all
Outputs:
- next_effects: float32 [8192], P(('chain', 'rec')), parts along dimension 0
- resid_sum: float32 [262144], P(('chain', 'ani')), parts along dimension 0
There are 2 independent parts, one for each index of `chain`. A program takes and returns all parts, laid end to end along the dimension named above; an argument that names none is the same for every part. Nothing has to cross between parts.
Inputs may be any that keep to these rules, and one draw needn't show every extreme that they name: `record_bin`: a record held by rec index k names a group of k * 2048 to (k + 1) * 2048 - 1.
All inputs are finite; a program needn't handle non-finite values. No bound on the sum of `accept` or of `live_records` on one device may be relied on, other than what follows from the above.
Results may differ from a plain program's by a relative error of at most 0.0033.
Values sent between devices are 32-bit elements; how exact they have to be, the bound alone decides.
A program may use at most 64 MiB of HBM per device.

v0:
```python
import math

import jax
import jax.numpy as jnp
from jax import lax
from jax.sharding import PartitionSpec as P

BLOCK = 128


def on_device(
    genotypes,
    effects,
    gaussian_draw,
    prior_prec,
    accept,
    herd_effect,
    phenotype,
    record_animal,
    record_bin,
    live_records,
):
    step_size = 0.005
    effects_half = effects.astype(jnp.bfloat16)
    partial_value = jnp.dot(genotypes, effects_half, preferred_element_type=jnp.float32)
    breeding_block = lax.psum(partial_value, "rec")
    breeding = lax.all_gather(breeding_block, "ani", axis=0, tiled=True)
    local_bin = record_bin - lax.axis_index("rec") * herd_effect.shape[0]
    position = jnp.arange(phenotype.shape[0], dtype=jnp.int32)
    live = position < live_records[0]
    herd_value = jnp.take(herd_effect, local_bin)
    residual = jnp.where(
        live, phenotype - herd_value - jnp.take(breeding, record_animal), jnp.zeros_like(phenotype)
    )
    animals = breeding.shape[0]
    partial_sums = jax.ops.segment_sum(residual, record_animal, num_segments=animals)
    share = lax.psum_scatter(partial_sums, "ani", scatter_dimension=0, tiled=True)
    resid_sum = lax.psum(share, "rec")
    resid_half = resid_sum.astype(jnp.bfloat16)
    grad_part = jnp.dot(resid_half, genotypes, preferred_element_type=jnp.float32)
    likelihood_grad = lax.psum(grad_part, "ani")
    gradient = likelihood_grad - prior_prec * effects
    proposal = effects + step_size * gradient + math.sqrt(2.0 * step_size) * gaussian_draw
    accepted = jnp.repeat(accept, BLOCK) == 1
    return (jnp.where(accepted, proposal, effects), resid_sum)


def solution(mesh):
    return jax.shard_map(
        on_device,
        mesh=mesh,
        in_specs=(
            P("ani", "rec"),
            P(("chain", "rec")),
            P(("chain", "rec")),
            P("rec"),
            P(("chain", "rec")),
            P(("chain", "rec")),
            P(("rec", "ani")),
            P(("rec", "ani")),
            P(("rec", "ani")),
            P(("rec", "ani")),
        ),
        out_specs=(P(("chain", "rec")), P(("chain", "ani"))),
        check_vma=False,
    )
```

profile of v0, /device:TPU:1, one launch (start us, length us, event | category | flops | bytes accessed | tf_op | source)
XLA Modules:
  0.0 464.9 jit_solution(7304369323534873181)
XLA Ops:
  7.2 0.0 copy-start
  7.2 0.0 copy-start.2
  7.2 0.0 all-reduce.5.cloned.1.call-start
  7.2 6.3 %fusion.4 = f32[1,32768]{1,0:T(1,128)} fusion(bf16[32768,128]{1,0:T(8,128)(2,1)} %param.10, f32[128]{0:T(128)} %param.11), kind=kOutput, calls=%fused_computation.13 | convolution fusion | flops 8388736 | bytes 8520192 | tf_op jit(solution)/shard_map/dot_general | solution.py:25
  13.5 0.0 all-reduce.5.cloned.1.call-update
  13.6 0.0 all-reduce.9.cloned.1.call-start
  14.3 0.0 copy-done.2
  14.3 0.0 copy-done
  14.3 0.0 copy-start.3
  14.3 45.5 %gather_fusion = f32[8192]{0:T(1024)S(1)} fusion(f32[2048]{0:T(1024)S(1)} %copy-done, s32[8192]{0:T(1024)S(1)} %fusion.3), kind=kCustom, calls=%fused_computation | custom fusion | bytes 98304 | tf_op jit(solution)/shard_map/jit(_take)/gather | solution.py:31
  59.9 0.0 copy-done.3
  59.9 95.9 %all-reduce.5.cloned.1.call-done = f32[32768]{0:T(1024)} async-done(((f32[32768]{0:T(1024)}), f32[32768]{0:T(1024)}) %all-reduce.5.cloned.1.call-update) | async-done | bytes 131088 | tf_op jit(solution)/shard_map/psum | solution.py:26
  155.8 12.2 %all_gather.3 = f32[131072]{0:T(1024)S(1)} all-gather(f32[32768]{0:T(1024)} %all-reduce.5.cloned.1.call-done), channel_id=1, replica_groups=mesh['rec'=32,'ani'=4,'chain'=2] {'ani'}, dimensions={0}, use_global_device_ids=true | all-gather | bytes 655360 | tf_op jit(solution)/shard_map/all_gather | solution.py:27
  167.9 0.0 copy-start.4
  167.9 0.0 copy-start.8
  167.9 45.5 %gather_fusion.1 = f32[8192]{0:T(1024)S(1)} fusion(f32[131072]{0:T(1024)S(1)} %all_gather.3, s32[8192]{0:T(1024)S(1)} %fusion.2), kind=kCustom, calls=%fused_computation.1 | custom fusion | bytes 98304 | tf_op jit(solution)/shard_map/jit(_take)/gather | solution.py:33
  213.5 0.0 copy-done.4
  213.5 44.0 %scatter_custom_fusion = f32[131072]{0:T(1024)} fusion(s32[8192]{0:T(1024)S(1)} %copy-done.3, f32[8192]{0:T(1024)S(1)} %subtract_select_fusion, f32[]{:T(128)} %constant.22.clone.1), kind=kCustom, calls=%fused_computation.4 | custom fusion | flops 8192 | bytes 524292 | tf_op jit(solution)/shard_map/scatter-add | solution.py:36
  257.5 0.0 all-reduce.9.cloned.1.call-update
  257.5 0.0 all-reduce.7.cloned.1.call-start
  257.6 0.0 copy-done.8
  257.6 0.6 dynamic-slice
  258.8 40.0 %all-reduce.9.cloned.1.call-done = f32[131072]{0:T(1024)} async-done(((f32[131072]{0:T(1024)}), f32[131072]{0:T(1024)}) %all-reduce.9.cloned.1.call-update) | async-done | bytes 524304
  298.8 1.6 dynamic-slice.1
  300.4 0.0 all-reduce.7.cloned.1.call-update
  301.0 140.5 %all-reduce.7.cloned.1.call-done = f32[32768]{0:T(1024)} async-done(((f32[32768]{0:T(1024)}), f32[32768]{0:T(1024)}) %all-reduce.7.cloned.1.call-update) | async-done | bytes 131088 | tf_op jit(solution)/shard_map/psum | solution.py:38
  441.6 0.9 convert_element_type.7
  442.5 0.1 reshape.47
  442.6 0.0 copy-start.5
  442.6 0.0 copy-start.6
  442.6 0.0 copy-start.7
  442.6 0.0 copy-start.1
  442.6 4.6 convolution_bitcast_fusion
  447.2 10.0 %psum.23 = f32[128]{0:T(128)S(1)} all-reduce(f32[128]{0:T(128)S(1)} %convolution_bitcast_fusion), channel_id=1, replica_groups=mesh['rec'=32,'ani'=4,'chain'=2] {'ani'}, use_global_device_ids=true, to_apply=%region_4.5 | all-reduce | flops 128 | bytes 1024 | tf_op jit(solution)/shard_map/psum | solution.py:41
  457.2 0.0 copy-done.5
  457.2 0.0 copy-done.6
  457.2 0.0 copy-done.7
  457.2 0.5 broadcast_select_fusion
  457.7 0.0 copy-done.1
  457.7 0.7 copy.17
  (3 shorter events, 0.1 us)
Async XLA Ops:
  7.2 7.1 %copy-start = (f32[2048]{0:T(1024)S(1)}, f32[2048]{0:T(1024)}, u32[]{:S(2)}) copy-start(f32[2048]{0:T(1024)} %param.15) | copy-start | bytes 24580
  7.2 7.1 %copy-start.2 = (s32[8192]{0:T(1024)S(1)}, s32[8192]{0:T(1024)}, u32[]{:S(2)}) copy-start(s32[8192]{0:T(1024)} %param.18) | copy-start | bytes 98308
  7.2 148.6 %all-reduce.5.cloned.1.call-start = ((), (), s32[]{:S(2)}) async-start(), calls=%async_computation | async-start | bytes 262144 | tf_op jit(solution)/shard_map/psum | solution.py:26
  13.6 285.2 %all-reduce.9.cloned.1.call-start = ((), (), s32[]{:S(2)}) async-start(), calls=%async_computation.2 | async-start | bytes 1048576
  14.3 45.6 %copy-start.3 = (s32[8192]{0:T(1024)S(1)}, s32[8192]{0:T(1024)}, u32[]{:S(2)}) copy-start(s32[8192]{0:T(1024)} %param.17) | copy-start | bytes 98308
  167.9 45.5 %copy-start.4 = (f32[8192]{0:T(1024)S(1)}, f32[8192]{0:T(1024)}, u32[]{:S(2)}) copy-start(f32[8192]{0:T(1024)} %param.16) | copy-start | bytes 98308
  167.9 89.6 %copy-start.8 = (u32[256]{0:T(256)S(1)}, u32[256]{0:T(256)}, u32[]{:S(2)}) copy-start(u32[256]{0:T(256)} %constant.51) | copy-start | bytes 3076
  257.5 184.1 %all-reduce.7.cloned.1.call-start = ((), (), s32[]{:S(2)}) async-start(), calls=%async_computation.1 | async-start | bytes 262144 | tf_op jit(solution)/shard_map/psum | solution.py:38
  442.6 14.6 %copy-start.5 = (f32[128]{0:T(128)S(1)}, f32[128]{0:T(128)}, u32[]{:S(2)}) copy-start(f32[128]{0:T(128)} %param.11) | copy-start | bytes 1540
  442.6 14.6 %copy-start.6 = (f32[128]{0:T(128)S(1)}, f32[128]{0:T(128)}, u32[]{:S(2)}) copy-start(f32[128]{0:T(128)} %param.12) | copy-start | bytes 1540
  442.6 14.6 %copy-start.7 = (f32[128]{0:T(128)S(1)}, f32[128]{0:T(128)}, u32[]{:S(2)}) copy-start(f32[128]{0:T(128)} %param.13) | copy-start | bytes 1540
  442.6 15.1 %copy-start.1 = (f32[32768]{0:T(1024)S(1)}, f32[32768]{0:T(1024)}, u32[]{:S(2)}) copy-start(f32[32768]{0:T(1024)} %all-reduce.7.cloned.1.call-done) | copy-start | bytes 393220
Sparse Core Ops, SparseCore 0:
  13.7 142.0 all-reduce.4
  257.6 41.1 all-reduce.8
  302.8 138.7 all-reduce.6
where the time goes:
time: 465 us
  waiting for transfers between devices  276 us (59%)
  local copies, waits for them, and re-layouts  94 us (20%)
  other arithmetic  45.5 us (10%)
  blocking collectives  22.1 us (5%)
  between operations  15.8 us (3%)
  matrix products  10.9 us (2%)
    psum x1, waiting for transfers between devices, on_device(): resid_sum = lax.psum(share, 'rec')  141 us
    psum x1, waiting for transfers between devices, on_device(): breeding_block = lax.psum(partial_value, 'rec')  95.9 us
    gather x1, local copies, waits for them, and re-layouts, on_device(): herd_value = jnp.take(herd_effect, local_bin)  45.5 us
    gather x1, local copies, waits for them, and re-layouts, on_device(): jnp.take(breeding, record_animal)  45.5 us
    scatter-add x1, other arithmetic, on_device(): jax.ops.segment_sum(residual, record_animal, num_segments=animals)  44 us
    unnamed x4, waiting for transfers between devices  40 us
    all_gather x1, blocking collectives, on_device(): breeding = lax.all_gather(breeding_block, 'ani', axis=0, tiled=True)  12.2 us
    psum x1, blocking collectives, on_device(): likelihood_grad = lax.psum(grad_part, 'ani')  9.98 us
  transfers between devices with their start and end apart: 3, of which 3 were waited for; matrix products, arithmetic and copies ran while one was open for 10% of the time, Pallas kernels for 0%

commit v1 on v0

v1 whole, which is shorter than its diff:
```python
import math

import jax
import jax.numpy as jnp
from jax import lax
from jax.experimental import pallas as pl
from jax.experimental.pallas import tpu as pltpu
from jax.sharding import PartitionSpec as P

BLOCK = 128
W = 1024
NX, NZ = 4, 8
F32, BF16 = jnp.float32, jnp.bfloat16


def row_kernel(first_ref, live_ref, phen_ref, animal_ref, bin_ref, herd_ref, out_ref):
    t = herd_ref[...]
    t1 = t.astype(BF16)
    r = t - t1.astype(F32)
    t2 = r.astype(BF16)
    t3 = (r - t2.astype(F32)).astype(BF16)
    table = jnp.concatenate([t1, t2, t3], axis=0)
    lo_iota = lax.broadcasted_iota(jnp.int32, (128, W), 0)
    hi_iota = lax.broadcasted_iota(jnp.int32, (16, W), 0)
    lane = lax.broadcasted_iota(jnp.int32, (1, W), 1)
    for i in range(phen_ref.shape[0]):
        b = bin_ref[i : i + 1, :] - first_ref[0]
        hi, lo = b >> 7, b & 127
        pick = jnp.where(lo_iota == lo, 1.0, 0.0).astype(BF16)
        g = jnp.dot(table, pick, preferred_element_type=F32)
        g = g[0:16] + g[16:32] + g[32:48]
        herd = jnp.sum(jnp.where(hi_iota == hi, g, 0.0), axis=0, keepdims=True)
        alive = lane + i * W < live_ref[0]
        out_ref[0, i : i + 1, :] = jnp.where(alive, phen_ref[i : i + 1, :] - herd, 0.0)
        out_ref[1, i : i + 1, :] = jnp.where(alive, animal_ref[i : i + 1, :], -1).astype(F32)


def scatter_kernel(first_ref, rec_ref, s_ref, n_ref, acc_ref):
    lo_iota = lax.broadcasted_iota(jnp.int32, (128, W), 0)
    hi_iota = lax.broadcasted_iota(jnp.int32, (256, W), 0)
    acc_ref[...] = jnp.zeros_like(acc_ref)

    def group(g, carry):
        for j in range(8):
            y = rec_ref[g, 0, j : j + 1, :]
            a = rec_ref[g, 1, j : j + 1, :].astype(jnp.int32) - first_ref[0]
            hi, lo = a >> 7, a & 127
            y1 = y.astype(BF16)
            y2 = y - y1.astype(F32)
            y1 = y1.astype(F32)
            rows = jnp.where(hi_iota == hi, 1.0, 0.0).astype(BF16)
            hit = lo_iota == lo
            cols = jnp.concatenate(
                [
                    jnp.where(hit, y1, 0.0).astype(BF16),
                    jnp.where(hit, y2, 0.0).astype(BF16),
                    jnp.where(hit, 1.0, 0.0).astype(BF16),
                ],
                axis=0,
            )
            acc_ref[...] += lax.dot_general(
                cols, rows, (((1,), (1,)), ((), ())), preferred_element_type=F32
            )
        return carry

    lax.fori_loop(0, rec_ref.shape[0], group, 0)
    s_ref[...] = (acc_ref[0:128] + acc_ref[128:256]).T
    n_ref[...] = acc_ref[256:384].T


def exchange_kernel(b_ref, s_ref, n_ref, out_ref, r1, part, r2, s1, v1, s2, v2, s3, v3, s4, v4):
    me = lax.axis_index("rec")
    mz, mx = me // NX, me % NX

    def at_x(d):
        return (mx + d) % NX

    def at_z(d):
        return (mz + d) % NZ

    barrier = pltpu.get_barrier_semaphore()
    for d in range(1, NX):
        pl.semaphore_signal(barrier, inc=1, device_id={"rec": mz * NX + at_x(d)})
    for d in range(1, NZ):
        pl.semaphore_signal(barrier, inc=1, device_id={"rec": at_z(d) * NX + mx})
    pl.semaphore_wait(barrier, NX - 1 + NZ - 1)

    ins = (b_ref, s_ref, n_ref)
    copies = []
    for d in (2, 1, 3):
        for k in range(3):
            copies.append(
                pltpu.make_async_remote_copy(
                    ins[k].at[at_x(d)], r1.at[d - 1, k], s1.at[d - 1, k], v1.at[d - 1, k],
                    device_id={"rec": mz * NX + at_x(d)},
                )
            )
            copies[-1].start()
    for c in copies:
        c.wait_recv()
    for k in range(3):
        part[:, k] = (ins[k][mx] + r1[0, k]) + (r1[1, k] + r1[2, k])
    for c in copies:
        c.wait_send()

    copies = []
    for d in (4, 3, 5, 2, 6, 1, 7):
        copies.append(
            pltpu.make_async_remote_copy(
                part.at[at_z(d)], r2.at[d - 1], s2.at[d - 1], v2.at[d - 1],
                device_id={"rec": at_z(d) * NX + mx},
            )
        )
        copies[-1].start()
    for c in copies:
        c.wait_recv()
    total = part[mz]
    for d in range(NZ - 1):
        total = total + r2[d]
    out_ref[mx, mz] = total[1] - total[2] * total[0]
    for c in copies:
        c.wait_send()

    copies = []
    for d in (4, 3, 5, 2, 6, 1, 7):
        copies.append(
            pltpu.make_async_remote_copy(
                out_ref.at[mx, mz], out_ref.at[mx, mz], s3.at[d - 1], v3.at[d - 1],
                device_id={"rec": at_z(d) * NX + mx},
            )
        )
        copies[-1].start()
    for d in range(1, NZ):
        pltpu.make_async_remote_copy(
            out_ref.at[mx, at_z(NZ - d)], out_ref.at[mx, at_z(NZ - d)], s3.at[d - 1], v3.at[d - 1],
            device_id={"rec": at_z(d) * NX + mx},
        ).wait_recv()
    for c in copies:
        c.wait_send()

    copies = []
    for d in (2, 1, 3):
        copies.append(
            pltpu.make_async_remote_copy(
                out_ref.at[mx], out_ref.at[mx], s4.at[d - 1], v4.at[d - 1],
                device_id={"rec": mz * NX + at_x(d)},
            )
        )
        copies[-1].start()
    for d in range(1, NX):
        pltpu.make_async_remote_copy(
            out_ref.at[at_x(NX - d)], out_ref.at[at_x(NX - d)], s4.at[d - 1], v4.at[d - 1],
            device_id={"rec": mz * NX + at_x(d)},
        ).wait_recv()
    for c in copies:
        c.wait_send()


VM = pl.BlockSpec(memory_space=pltpu.VMEM)
SM = pl.BlockSpec(memory_space=pltpu.SMEM)


def shape(*dims):
    return jax.ShapeDtypeStruct(dims, F32)


def on_device(
    genotypes, effects, gaussian_draw, prior_prec, accept,
    herd_effect, phenotype, record_animal, record_bin, live_records,
):
    step_size = 0.005
    rd, own = phenotype.shape[0], genotypes.shape[0]
    first_bin = (lax.axis_index("rec") * herd_effect.shape[0]).astype(jnp.int32).reshape(1)
    first_animal = (lax.axis_index("ani") * own).astype(jnp.int32).reshape(1)
    rows = pl.pallas_call(
        row_kernel,
        out_shape=shape(2, rd // W, W),
        in_specs=[SM, SM, VM, VM, VM, VM],
        out_specs=VM,
    )(
        first_bin, live_records, phenotype.reshape(-1, W), record_animal.reshape(-1, W),
        record_bin.reshape(-1, W), herd_effect.reshape(16, 128),
    )
    records = lax.all_gather(rows, "ani", axis=0)
    breeding = jnp.dot(genotypes, effects.astype(BF16), preferred_element_type=F32)
    s, n = pl.pallas_call(
        scatter_kernel,
        out_shape=(shape(own // 128, 128), shape(own // 128, 128)),
        in_specs=[SM, VM],
        out_specs=(VM, VM),
        scratch_shapes=[pltpu.VMEM((384, 256), F32)],
    )(first_animal, records)
    dma = pltpu.SemaphoreType.DMA
    part = (NX, NZ, 8, 128)
    resid_sum = pl.pallas_call(
        exchange_kernel,
        out_shape=shape(*part),
        in_specs=[VM, VM, VM],
        out_specs=VM,
        scratch_shapes=[
            pltpu.VMEM((NX - 1, 3, NZ, 8, 128), F32),
            pltpu.VMEM((NZ, 3, 8, 128), F32),
            pltpu.VMEM((NZ - 1, 3, 8, 128), F32),
            dma((NX - 1, 3)), dma((NX - 1, 3)),
            dma((NZ - 1,)), dma((NZ - 1,)),
            dma((NZ - 1,)), dma((NZ - 1,)),
            dma((NX - 1,)), dma((NX - 1,)),
        ],
        compiler_params=pltpu.CompilerParams(collective_id=0, has_side_effects=True),
    )(breeding.reshape(part), s.reshape(part), n.reshape(part)).reshape(own)
    grad_part = jnp.dot(resid_sum.astype(BF16), genotypes, preferred_element_type=F32)
    gradient = lax.psum(grad_part, "ani") - prior_prec * effects
    proposal = effects + step_size * gradient + math.sqrt(2.0 * step_size) * gaussian_draw
    accepted = jnp.repeat(accept, BLOCK) == 1
    return (jnp.where(accepted, proposal, effects), resid_sum)


def solution(mesh):
    return jax.shard_map(
        on_device,
        mesh=mesh,
        in_specs=(
            P("ani", "rec"),
            P(("chain", "rec")),
            P(("chain", "rec")),
            P("rec"),
            P(("chain", "rec")),
            P(("chain", "rec")),
            P(("rec", "ani")),
            P(("rec", "ani")),
            P(("rec", "ani")),
            P(("rec", "ani")),
        ),
        out_specs=(P(("chain", "rec")), P(("chain", "ani"))),
        check_vma=False,
    )
```

time: 465 us -> 75.5 us (0.16)
  waiting for transfers between devices: 276 us -> 0 us
  local copies, waits for them, and re-layouts: 94 us -> 4.89 us
  other arithmetic: 45.5 us -> 1.43 us
  Pallas kernels: 0 us -> 37.7 us
  between operations: 15.8 us -> 2.01 us
    psum x2 -> x0, waiting for transfers between devices: 236 us -> none  [the longest x1 141 us: on_device(): resid_sum = lax.psum(share, 'rec')]
    gather x2 -> x0, local copies, waits for them, and re-layouts: 91.1 us -> none  [the longest x1 45.5 us: on_device(): herd_value = jnp.take(herd_effect, local_bin)]
    scatter-add x1 -> x0, other arithmetic: 44 us -> none  [on_device(): jax.ops.segment_sum(residual, record_animal, num_segments=animals)]
    unnamed x4 -> x0, waiting for transfers between devices: 40 us -> none
    pallas_call x0 -> x3, Pallas kernels: none -> 37.7 us  [the longest x1 26.1 us: on_device(): pl.pallas_call(exchange_kernel, out_shape=shape(*part), in_specs=[VM, VM,...]
  transfers between devices with their start and end apart: 3 -> 0, of which waited for: 3 -> 0; matrix products, arithmetic and copies ran while one was open for 10% -> 0% of each run, Pallas kernels for 0% -> 0%
where the time goes in v1:
time: 75.5 us; the launch traced here: 75 us
  Pallas kernels  37.7 us (50%)
  blocking collectives  18 us (24%)
  matrix products  10.9 us (14%)
  local copies, waits for them, and re-layouts  4.89 us (6%)
  between operations  2.01 us (3%)
  other arithmetic  1.43 us (2%)
    pallas_call x1, Pallas kernels, on_device(): pl.pallas_call(exchange_kernel, out_shape=shape(*part), in_specs=[VM, VM,...  26.1 us
    pallas_call x1, Pallas kernels, on_device(): pl.pallas_call(scatter_kernel, out_shape=(shape(own // 128, 128), shape(o...  9.49 us
    all_gather x1, blocking collectives, on_device(): records = lax.all_gather(rows, 'ani', axis=0)  9.46 us
    psum x1, blocking collectives, on_device(): gradient = lax.psum(grad_part, 'ani') - prior_prec * effects  8.56 us
    dot_general x1, matrix products, on_device(): jnp.dot(genotypes, effects.astype(BF16), preferred_element_type=F32)  6.31 us
    dot_general x1, matrix products, on_device(): jnp.dot(resid_sum.astype(BF16), genotypes, preferred_element_type=F32)  4.62 us
    pallas_call x1, Pallas kernels, on_device(): pl.pallas_call(row_kernel, out_shape=shape(2, rd // W, W), in_specs=[SM,...  2.18 us

profile of v1, /device:TPU:1, one launch (start us, length us, event | category | flops | bytes accessed | tf_op | source)
XLA Modules:
  0.0 75.0 jit_solution(10219211421557225110)
XLA Ops:
  0.6 1.4 %reshape.41.phen_ref = f32[8,1024]{1,0:T(8,128)} reshape(f32[8192]{0:T(1024)} %param.16) | data formatting | bytes 65536 | tf_op jit(solution)/shard_map/reshape | solution.py:181
  2.0 1.4 %reshape.42.animal_ref = s32[8,1024]{1,0:T(8,128)} reshape(s32[8192]{0:T(1024)} %param.17) | data formatting | bytes 65536 | tf_op jit(solution)/shard_map/reshape | solution.py:181
  3.4 1.4 %reshape.43.bin_ref = s32[8,1024]{1,0:T(8,128)} reshape(s32[8192]{0:T(1024)} %param.18) | data formatting | bytes 65536 | tf_op jit(solution)/shard_map/reshape | solution.py:182
  5.4 2.2 %shard_map.113 = f32[2,8,1024]{2,1,0:T(8,128)} custom-call(s32[1]{0:T(128)} %bitcast.5.first_ref, s32[1]{0:T(128)S(6)} %copy.14.live_ref, f32[8,1024]{1,0:T(8,128)} %reshape.41.phen_ref, s32[8,1024]{1,0:T(8,128)} %reshape.42.animal_ref, s32[8,1024]{1,0:T(8,128)} %reshape.43.bin_ref, f32[16,128]{1,0:T(8,128)} %bitcast.25), custom_call_target="tpu_custom_call" | custom-call | tf_op jit(solution)/shard_map/pallas_call | solution.py:175
  7.6 9.5 %all-gather = f32[8,8,1024]{2,1,0:T(8,128)} all-gather(f32[2,8,1024]{2,1,0:T(8,128)} %shard_map.113), channel_id=2, replica_groups=mesh['rec'=32,'ani'=4,'chain'=2] {'ani'}, dimensions={0}, use_global_device_ids=true | all-gather | bytes 327680 | tf_op jit(solution)/shard_map/all_gather | solution.py:184
  17.1 9.5 %shard_map.114 = (f32[256,128]{1,0:T(8,128)}, f32[256,128]{1,0:T(8,128)}) custom-call(s32[1]{0:T(128)} %bitcast.4.first_ref, f32[4,2,8,1024]{3,2,1,0:T(8,128)} %bitcast.21), custom_call_target="tpu_custom_call" | custom-call | tf_op jit(solution)/shard_map/pallas_call | solution.py:186
  26.5 6.3 %fusion = f32[1,32768]{1,0:T(1,128)} fusion(bf16[32768,128]{1,0:T(8,128)(2,1)} %param.10, f32[128]{0:T(128)} %param.11), kind=kOutput, calls=%fused_computation.2 | convolution fusion | flops 8388736 | bytes 8520192 | tf_op jit(solution)/shard_map/dot_general | solution.py:185
  32.9 26.1 %shard_map.115 = f32[4,8,8,128]{3,2,1,0:T(8,128)} custom-call(f32[4,8,8,128]{3,2,1,0:T(8,128)} %bitcast.22, f32[4,8,8,128]{3,2,1,0:T(8,128)} %bitcast.23, f32[4,8,8,128]{3,2,1,0:T(8,128)} %bitcast.24), custom_call_target="tpu_custom_call" | custom-call | tf_op jit(solution)/shard_map/pallas_call | solution.py:195
  58.9 0.9 %convert_element_type.7 = bf16[32768]{0:T(1024)(128)(2,1)S(1)} convert(f32[32768]{0:T(1024)} %bitcast.19) | non-fusion elementwise | flops 32768 | bytes 196608 | tf_op jit(solution)/shard_map/convert_element_type | solution.py:211
  59.8 0.1 reshape.51
  59.9 0.0 copy-start.1
  59.9 0.0 copy-start.2
  59.9 0.0 copy-start.3
  60.0 0.0 copy-start
  60.0 4.6 %convolution_bitcast_fusion = f32[128]{0:T(128)S(1)} fusion(bf16[32768,1]{0,1:T(2,128)(2,1)S(1)} %reshape.51, bf16[32768,128]{1,0:T(8,128)(2,1)} %param.10), kind=kOutput, calls=%fused_computation | convolution fusion | flops 8388608 | bytes 8454656 | tf_op jit(solution)/shard_map/dot_general | solution.py:211
  64.6 8.6 %psum.7 = f32[128]{0:T(128)S(1)} all-reduce(f32[128]{0:T(128)S(1)} %convolution_bitcast_fusion), channel_id=1, replica_groups=mesh['rec'=32,'ani'=4,'chain'=2] {'ani'}, use_global_device_ids=true, to_apply=%region_0.0 | all-reduce | flops 128 | bytes 1024 | tf_op jit(solution)/shard_map/psum | solution.py:212
  73.8 0.0 copy-done.1
  73.8 0.0 copy-done.2
  73.8 0.0 copy-done.3
  73.8 0.5 broadcast_select_fusion
  74.3 0.0 copy-done
  74.4 0.7 copy.15
Async XLA Ops:
  59.9 13.9 %copy-start.1 = (f32[128]{0:T(128)S(1)}, f32[128]{0:T(128)}, u32[]{:S(2)}) copy-start(f32[128]{0:T(128)} %param.11) | copy-start | bytes 1540
  59.9 13.9 %copy-start.2 = (f32[128]{0:T(128)S(1)}, f32[128]{0:T(128)}, u32[]{:S(2)}) copy-start(f32[128]{0:T(128)} %param.12) | copy-start | bytes 1540
  59.9 13.9 %copy-start.3 = (f32[128]{0:T(128)S(1)}, f32[128]{0:T(128)}, u32[]{:S(2)}) copy-start(f32[128]{0:T(128)} %param.13) | copy-start | bytes 1540
  60.0 14.4 %copy-start = (f32[4,8,8,128]{3,2,1,0:T(8,128)S(1)}, f32[4,8,8,128]{3,2,1,0:T(8,128)}, u32[]{:S(2)}) copy-start(f32[4,8,8,128]{3,2,1,0:T(8,128)} %shard_map.115) | copy-start | bytes 393220

commit v2 on v1

--- a/solution.py
+++ b/solution.py
@@ -9,6 +9,7 @@
 
 BLOCK = 128
 W = 1024
+NA = 4
 NX, NZ = 4, 8
 F32, BF16 = jnp.float32, jnp.bfloat16
 
@@ -164,6 +165,49 @@
     return jax.ShapeDtypeStruct(dims, F32)
 
 
+def greet(me, n):
+    barrier = pltpu.get_barrier_semaphore()
+    for d in range(1, n):
+        pl.semaphore_signal(barrier, inc=1, device_id={"ani": (me + d) % n})
+    pl.semaphore_wait(barrier, n - 1)
+
+
+def spread_kernel(in_ref, out_ref, send, recv):
+    n = out_ref.shape[0]
+    me = lax.axis_index("ani")
+    greet(me, n)
+    copies = []
+    for d in range(1, n):
+        copies.append(
+            pltpu.make_async_remote_copy(
+                in_ref, out_ref.at[me], send.at[d - 1], recv.at[d - 1],
+                device_id={"ani": (me + d) % n},
+            )
+        )
+        copies[-1].start()
+    out_ref[me] = in_ref[...]
+    for d in range(1, n):
+        src = (me + n - d) % n
+        pltpu.make_async_remote_copy(
+            in_ref, out_ref.at[src], send.at[d - 1], recv.at[d - 1],
+            device_id={"ani": (me + d) % n},
+        ).wait_recv()
+    for c in copies:
+        c.wait_send()
+
+
+def spread(x, collective_id):
+    n = NA
+    return pl.pallas_call(
+        spread_kernel,
+        out_shape=shape(n, *x.shape),
+        in_specs=[VM],
+        out_specs=VM,
+        scratch_shapes=[pltpu.SemaphoreType.DMA((n - 1,)), pltpu.SemaphoreType.DMA((n - 1,))],
+        compiler_params=pltpu.CompilerParams(collective_id=collective_id, has_side_effects=True),
+    )(x)
+
+
 def on_device(
     genotypes, effects, gaussian_draw, prior_prec, accept,
     herd_effect, phenotype, record_animal, record_bin, live_records,
@@ -181,7 +225,7 @@
         first_bin, live_records, phenotype.reshape(-1, W), record_animal.reshape(-1, W),
         record_bin.reshape(-1, W), herd_effect.reshape(16, 128),
     )
-    records = lax.all_gather(rows, "ani", axis=0)
+    records = spread(rows, 1)
     breeding = jnp.dot(genotypes, effects.astype(BF16), preferred_element_type=F32)
     s, n = pl.pallas_call(
         scatter_kernel,
@@ -209,7 +253,8 @@
         compiler_params=pltpu.CompilerParams(collective_id=0, has_side_effects=True),
     )(breeding.reshape(part), s.reshape(part), n.reshape(part)).reshape(own)
     grad_part = jnp.dot(resid_sum.astype(BF16), genotypes, preferred_element_type=F32)
-    gradient = lax.psum(grad_part, "ani") - prior_prec * effects
+    g = spread(jnp.broadcast_to(grad_part, (8, 128)), 2)[:, 0]
+    gradient = (g[0] + g[1]) + (g[2] + g[3]) - prior_prec * effects
     proposal = effects + step_size * gradient + math.sqrt(2.0 * step_size) * gaussian_draw
     accepted = jnp.repeat(accept, BLOCK) == 1
     return (jnp.where(accepted, proposal, effects), resid_sum)

time: 75.5 us -> 76.1 us (level)
  blocking collectives: 18 us -> 0 us
  Pallas kernels: 37.7 us -> 54.9 us
    pallas_call x0 -> x2, Pallas kernels: none -> 18 us  [spread(): pl.pallas_call(spread_kernel, out_shape=shape(n, *x.shape), in_specs=[VM]...]
    all_gather x1 -> x0, blocking collectives: 9.46 us -> none  [on_device(): records = lax.all_gather(rows, 'ani', axis=0)]
    psum x1 -> x0, blocking collectives: 8.56 us -> none  [on_device(): gradient = lax.psum(grad_part, 'ani') - prior_prec * effects]
where the time goes in v2:
time: 76.1 us; the launch traced here: 75.5 us
  Pallas kernels  54.9 us (72%)
  matrix products  10.9 us (14%)
  local copies, waits for them, and re-layouts  5.5 us (7%)
  other arithmetic  2.13 us (3%)
  between operations  2.03 us (3%)
    pallas_call x1, Pallas kernels, on_device(): pl.pallas_call(exchange_kernel, out_shape=shape(*part), in_specs=[VM, VM,...  25.3 us
    pallas_call x2, Pallas kernels, spread(): pl.pallas_call(spread_kernel, out_shape=shape(n, *x.shape), in_specs=[VM]...  18 us
    pallas_call x1, Pallas kernels, on_device(): pl.pallas_call(scatter_kernel, out_shape=(shape(own // 128, 128), shape(o...  9.48 us
    dot_general x1, matrix products, on_device(): jnp.dot(genotypes, effects.astype(BF16), preferred_element_type=F32)  6.31 us
    dot_general x1, matrix products, on_device(): jnp.dot(resid_sum.astype(BF16), genotypes, preferred_element_type=F32)  4.62 us
    pallas_call x1, Pallas kernels, on_device(): pl.pallas_call(row_kernel, out_shape=shape(2, rd // W, W), in_specs=[SM,...  2.18 us

profile of v2, /device:TPU:1, one launch (start us, length us, event | category | flops | bytes accessed | tf_op | source)
XLA Modules:
  0.0 75.5 jit_solution(12341423577011102529)
XLA Ops:
  0.6 1.4 %reshape.52.phen_ref = f32[8,1024]{1,0:T(8,128)} reshape(f32[8192]{0:T(1024)} %param.16) | data formatting | bytes 65536 | tf_op jit(solution)/shard_map/reshape | solution.py:225
  2.0 1.4 %reshape.53.animal_ref = s32[8,1024]{1,0:T(8,128)} reshape(s32[8192]{0:T(1024)} %param.17) | data formatting | bytes 65536 | tf_op jit(solution)/shard_map/reshape | solution.py:225
  3.4 1.4 %reshape.54.bin_ref = s32[8,1024]{1,0:T(8,128)} reshape(s32[8192]{0:T(1024)} %param.18) | data formatting | bytes 65536 | tf_op jit(solution)/shard_map/reshape | solution.py:226
  5.4 2.2 %shard_map.113.in_ref = f32[2,8,1024]{2,1,0:T(8,128)} custom-call(s32[1]{0:T(128)} %bitcast.5.first_ref, s32[1]{0:T(128)S(6)} %copy.14.live_ref, f32[8,1024]{1,0:T(8,128)} %reshape.52.phen_ref, s32[8,1024]{1,0:T(8,128)} %reshape.53.animal_ref, s32[8,1024]{1,0:T(8,128)} %reshape.54.bin_ref, f32[16,128]{1,0:T(8,128)} %bitcast.33), custom_call_target="tpu_custom_call" | custom-call | tf_op jit(solution)/shard_map/pallas_call | solution.py:219
  7.6 9.9 %shard_map.114.rec_ref = f32[4,2,8,1024]{3,2,1,0:T(8,128)} custom-call(f32[2,8,1024]{2,1,0:T(8,128)} %shard_map.113.in_ref), custom_call_target="tpu_custom_call" | custom-call | tf_op jit(solution)/shard_map/pallas_call | solution.py:201
  17.5 9.5 %shard_map.115 = (f32[256,128]{1,0:T(8,128)}, f32[256,128]{1,0:T(8,128)}) custom-call(s32[1]{0:T(128)} %bitcast.4.first_ref, f32[4,2,8,1024]{3,2,1,0:T(8,128)} %shard_map.114.rec_ref), custom_call_target="tpu_custom_call" | custom-call | tf_op jit(solution)/shard_map/pallas_call | solution.py:230
  27.0 6.3 %fusion.3 = f32[1,32768]{1,0:T(1,128)} fusion(bf16[32768,128]{1,0:T(8,128)(2,1)} %param.10, f32[128]{0:T(128)} %param.11), kind=kOutput, calls=%fused_computation.6 | convolution fusion | flops 8388736 | bytes 8520192 | tf_op jit(solution)/shard_map/dot_general | solution.py:229
  33.3 25.3 %shard_map.116 = f32[4,8,8,128]{3,2,1,0:T(8,128)} custom-call(f32[4,8,8,128]{3,2,1,0:T(8,128)} %bitcast.30, f32[4,8,8,128]{3,2,1,0:T(8,128)} %bitcast.31, f32[4,8,8,128]{3,2,1,0:T(8,128)} %bitcast.32), custom_call_target="tpu_custom_call" | custom-call | tf_op jit(solution)/shard_map/pallas_call | solution.py:239
  58.6 0.9 %convert_element_type.7 = bf16[32768]{0:T(1024)(128)(2,1)S(1)} convert(f32[32768]{0:T(1024)} %bitcast.28) | non-fusion elementwise | flops 32768 | bytes 196608 | tf_op jit(solution)/shard_map/convert_element_type | solution.py:255
  59.5 0.1 reshape.61
  59.6 0.0 copy-start.1
  59.6 0.0 copy-start.2
  59.6 0.0 copy-start.3
  59.6 0.0 copy-start
  59.7 4.6 %convolution_bitcast_fusion = f32[128]{0:T(128)S(1)} fusion(bf16[32768,1]{0,1:T(2,128)(2,1)S(1)} %reshape.61, bf16[32768,128]{1,0:T(8,128)(2,1)} %param.10), kind=kOutput, calls=%fused_computation | convolution fusion | flops 8388608 | bytes 8454656 | tf_op jit(solution)/shard_map/dot_general | solution.py:255
  64.3 0.6 broadcast_in_dim.4.in_ref
  64.9 8.1 %shard_map.117 = f32[4,8,128]{2,1,0:T(8,128)} custom-call(f32[8,128]{1,0:T(8,128)} %broadcast_in_dim.4.in_ref), custom_call_target="tpu_custom_call" | custom-call | tf_op jit(solution)/shard_map/pallas_call | solution.py:201
  73.6 0.0 copy-done.1
  73.6 0.0 copy-done.2
  73.6 0.0 copy-done.3
  73.6 1.2 %broadcast_select_fusion = f32[128]{0:T(128)} fusion(f32[128]{0:T(128)S(1)} %copy-done.1, pred[]{:T(512)} %bitcast, f32[128]{0:T(128)S(1)} %copy-done.2, f32[128]{0:T(128)S(1)} %copy-done.3, f32[4,8,128]{2,1,0:T(8,128)} %shard_map.117), kind=kLoop, calls=%fused_computation.1 | loop fusion | flops 1280 | bytes 4097 | tf_op jit(solution)/shard_map/jit(_where)/select_n | solution.py:260
  74.9 0.0 copy-done
  74.9 0.7 copy.15
Async XLA Ops:
  59.6 14.0 %copy-start.1 = (f32[128]{0:T(128)S(1)}, f32[128]{0:T(128)}, u32[]{:S(2)}) copy-start(f32[128]{0:T(128)} %param.11) | copy-start | bytes 1540
  59.6 14.0 %copy-start.2 = (f32[128]{0:T(128)S(1)}, f32[128]{0:T(128)}, u32[]{:S(2)}) copy-start(f32[128]{0:T(128)} %param.12) | copy-start | bytes 1540
  59.6 14.0 %copy-start.3 = (f32[128]{0:T(128)S(1)}, f32[128]{0:T(128)}, u32[]{:S(2)}) copy-start(f32[128]{0:T(128)} %param.13) | copy-start | bytes 1540
  59.6 15.2 %copy-start = (f32[4,8,8,128]{3,2,1,0:T(8,128)S(1)}, f32[4,8,8,128]{3,2,1,0:T(8,128)}, u32[]{:S(2)}) copy-start(f32[4,8,8,128]{3,2,1,0:T(8,128)} %shard_map.116) | copy-start | bytes 393220
